TPU v7x, 256 devices: a whole 4x4x8 slice. The times are simulated.
256 devices in a mesh: ctx: 32 (over z, x), rep: 8 (over y, core).
Axes of the slice: x: 4, y: 4, z: 8, core: 2. Of those that a mesh axis runs over, the one named last changes fastest.
Arguments:
- query: bfloat16 [32768, 2048], P(('rep', 'ctx')), parts along dimension 0, may hold values from -6 to 6
- key: bfloat16 [32768, 2048], P(('rep', 'ctx')), parts along dimension 0, may hold values from -6 to 6
- value: bfloat16 [32768, 2048], P(('rep', 'ctx')), parts along dimension 0, may hold values from -6 to 6
- beta: float32 [32768, 16], P(('rep', 'ctx')), parts along dimension 0, may hold values from 0.05 to 0.95
- log_gate: float32 [32768, 16], P(('rep', 'ctx')), parts along dimension 0, may hold values from -1.5 to 0
- level_weight: float32 [32768, 16, 6], P(('rep', 'ctx')), parts along dimension 0, may hold values from 0.1 to 1.5
- norm_gain: float32 [128], replicated, may hold values from 0.5 to 1.5
- grad_out: bfloat16 [32768, 2048], P(('rep', 'ctx')), parts along dimension 0, may hold values from -6 to 6
- grad_final_state: float32 [16384, 128], P(('rep', 'ctx')), parts along dimension 0, may hold values from -6 to 6
Outputs:
- grad_query: bfloat16 [32768, 2048], P(('rep', 'ctx')), parts along dimension 0
- grad_key: bfloat16 [32768, 2048], P(('rep', 'ctx')), parts along dimension 0
- grad_value: bfloat16 [32768, 2048], P(('rep', 'ctx')), parts along dimension 0
- grad_beta: float32 [32768, 16], P(('rep', 'ctx')), parts along dimension 0
- grad_level: float32 [32768, 16, 6], P(('rep', 'ctx')), parts along dimension 0
- grad_gain: float32 [1024], P('rep'), parts along dimension 0
- final_state: float32 [16384, 128], P(('rep', 'ctx')), parts along dimension 0
There are 8 independent parts, one for each index of `rep`. A program takes and returns all parts, laid end to end along the dimension named above; an argument that names none is the same for every part. Nothing has to cross between parts.
All inputs are finite; a program needn't handle non-finite values.
Results may differ from a plain program's by a relative error of at most 0.001.
Values sent between devices are 32-bit elements; how exact they have to be, the bound alone decides.
No kernel may reach another device: no remote copies, remote signals or barrier semaphores. Data moves between devices by JAX's collectives and lax.ppermute only.
A program may use at most 128 MiB of HBM per device.

v0:
```python
import jax
import jax.numpy as jnp
from jax import lax
from jax.sharding import PartitionSpec as P

epsilon = 1e-06
topmost_level = lax.Precision.HIGHEST


def from_partner(value, axis, bit):
    mask = 2**bit
    pairs = [(source, source ^ mask) for source in range(lax.axis_size(axis))]
    return lax.ppermute(value, axis, pairs)


def normalize(values):
    return values * lax.rsqrt(jnp.sum(values * values, axis=-1, keepdims=True) + epsilon)


def split_heads(values, head_count):
    row_count = values.shape[0]
    return values.reshape(row_count, head_count, -1).transpose(1, 0, 2)


def prepare(query, key, value, beta, cum_gate):
    head_count = cum_gate.shape[0]
    row_count = cum_gate.shape[1]
    query_normed = normalize(split_heads(query, head_count))
    normalized_key = normalize(split_heads(key, head_count))
    value_heads = split_heads(value, head_count)
    beta_heads = beta.T
    strict = jnp.tril(jnp.ones((row_count, row_count), dtype=bool), -1)
    log_gaps = cum_gate[:, :, None] - cum_gate[:, None, :]
    decays = jnp.exp(jnp.where(strict[None], log_gaps, -jnp.inf))
    key_inner = jnp.einsum("htk,hsk->hts", normalized_key, normalized_key, precision=topmost_level)
    system = (
        jnp.eye(row_count, dtype=cum_gate.dtype)[None] + beta_heads[:, :, None] * decays * key_inner
    )
    surrogate_value = jax.scipy.linalg.solve_triangular(
        system, beta_heads[:, :, None] * value_heads, lower=True
    )
    trailing_decay = jnp.exp(cum_gate[:, -1:] - cum_gate)
    state_per_block = jnp.einsum(
        "fni,fnb->fib",
        normalized_key * trailing_decay[:, :, None],
        surrogate_value,
        precision=topmost_level,
    )
    return (query_normed, normalized_key, surrogate_value, state_per_block)


def finish(
    query_normed, normalized_key, surrogate_value, level_weight, norm_gain, bucket_states, cum_gate
):
    row_count = cum_gate.shape[1]
    inclusive = jnp.tril(jnp.ones((row_count, row_count), dtype=bool))
    log_gaps = cum_gate[:, :, None] - cum_gate[:, None, :]
    decays = jnp.exp(jnp.where(inclusive[None], log_gaps, -jnp.inf))
    attention_scores = (
        jnp.einsum("htk,hsk->hts", query_normed, normalized_key, precision=topmost_level) * decays
    )
    intra_out = jnp.einsum(
        "hts,hsv->htv", attention_scores, surrogate_value, precision=topmost_level
    )
    cross_out = jnp.einsum("htk,lhkv->lhtv", query_normed, bucket_states, precision=topmost_level)
    level_heads = level_weight.transpose(1, 0, 2)
    weighted = level_heads[:, :, 1:] * jnp.exp(cum_gate)[:, :, None]
    mixture = level_heads[:, :, 0:1] * intra_out + jnp.einsum(
        "htl,lhtv->htv", weighted, cross_out, precision=topmost_level
    )
    inverse_rms = lax.rsqrt(jnp.mean(mixture * mixture, axis=-1, keepdims=True) + epsilon)
    normed = mixture * inverse_rms * norm_gain
    return normed.transpose(1, 0, 2).reshape(row_count, -1)


def local(query, key, value, beta, log_gate, level_weight, norm_gain, grad_out, grad_final_state):
    levels = level_weight.shape[2]
    cum_gate = jnp.cumsum(log_gate.T, axis=1)
    block_grand_total = cum_gate[:, -1]

    def local_prepare(query_float, key_float, value_float, beta_float):
        return prepare(query_float, key_float, value_float, beta_float, cum_gate)

    prepared, prepare_back = jax.vjp(
        local_prepare,
        query.astype(jnp.float32),
        key.astype(jnp.float32),
        value.astype(jnp.float32),
        beta,
    )
    query_normed, normalized_key, surrogate_value, state_per_block = prepared
    device = lax.axis_index("ctx")
    aggregate = state_per_block
    group_total = block_grand_total
    offset = jnp.zeros_like(block_grand_total)
    records = []
    bucket_list = []
    for degree in range(levels - 1):
        is_upper = device >> degree & 1 == 1
        if degree < levels - 2:
            partner, partner_total = from_partner((aggregate, group_total), "ctx", degree)
        else:
            partner, partner_total = from_partner((aggregate, group_total), "ctx", degree)
        bucket_list.append(jnp.where(is_upper, jnp.exp(offset)[:, None, None] * partner, 0.0))
        records.append((is_upper, offset, group_total, partner_total))
        aggregate = jnp.where(
            is_upper,
            jnp.exp(group_total)[:, None, None] * partner + aggregate,
            jnp.exp(partner_total)[:, None, None] * aggregate + partner,
        )
        offset = jnp.where(is_upper, offset + partner_total, offset)
        group_total = group_total + partner_total
    bucket_stack = jnp.stack(bucket_list)
    rows_dev = grad_final_state.shape[0]
    rows_total = aggregate.shape[0] * aggregate.shape[1]
    full_rows = aggregate.reshape(rows_total, -1)
    own_rows = lax.dynamic_slice_in_dim(full_rows, device * rows_dev, rows_dev, 0)

    def local_finish(normed_queries, normed_keys, pseudo_rows, level_rows, gain_rows, bucket_rows):
        return finish(
            normed_queries, normed_keys, pseudo_rows, level_rows, gain_rows, bucket_rows, cum_gate
        )

    mixed_out, finish_back = jax.vjp(
        local_finish,
        query_normed,
        normalized_key,
        surrogate_value,
        level_weight,
        norm_gain,
        bucket_stack,
    )
    grad_qnormed, grad_knormed, grad_pseudo, grad_level, grad_gain_local, grad_buckets = (
        finish_back(grad_out.astype(jnp.float32))
    )
    seed_rows = lax.dynamic_update_slice_in_dim(
        jnp.zeros((rows_total, grad_final_state.shape[1]), jnp.float32),
        grad_final_state,
        device * rows_dev,
        0,
    )
    adjoint = seed_rows.reshape(state_per_block.shape)
    for degree in reversed(range(levels - 1)):
        is_upper, offset, group_total, partner_total = records[degree]
        outgoing = jnp.where(
            is_upper,
            jnp.exp(offset)[:, None, None] * grad_buckets[degree]
            + jnp.exp(group_total)[:, None, None] * adjoint,
            adjoint,
        )
        retained = jnp.where(is_upper, adjoint, jnp.exp(partner_total)[:, None, None] * adjoint)
        incoming = from_partner(outgoing, "ctx", degree)
        adjoint = retained + incoming
    grad_query, grad_key, grad_value, grad_beta = prepare_back(
        (grad_qnormed, grad_knormed, grad_pseudo, adjoint)
    )
    grad_gain = lax.psum(grad_gain_local, "ctx")
    return (
        grad_query.astype(jnp.bfloat16),
        grad_key.astype(jnp.bfloat16),
        grad_value.astype(jnp.bfloat16),
        grad_beta,
        grad_level,
        grad_gain,
        own_rows,
    )


def solution(mesh):
    in_specs = (
        P(("rep", "ctx"), None),
        P(("rep", "ctx"), None),
        P(("rep", "ctx"), None),
        P(("rep", "ctx"), None),
        P(("rep", "ctx"), None),
        P(("rep", "ctx"), None, None),
        P(),
        P(("rep", "ctx"), None),
        P(("rep", "ctx"), None),
    )
    out_specs = (
        P(("rep", "ctx"), None),
        P(("rep", "ctx"), None),
        P(("rep", "ctx"), None),
        P(("rep", "ctx"), None),
        P(("rep", "ctx"), None, None),
        P("rep"),
        P(("rep", "ctx"), None),
    )
    return jax.shard_map(local, mesh=mesh, in_specs=in_specs, out_specs=out_specs, check_vma=False)
```

profile of v0, /device:TPU:16, one launch (start us, length us, event | category | flops | bytes accessed | tf_op | source)
XLA Modules:
  0.0 612.7 jit_solution(5073137040125510307)
XLA Ops:
  8.1 157.8 %custom-call.7 = f32[16,1,128,128]{2,3,1,0:T(8,128)} custom-call(f32[16,1,128,128]{3,2,1,0:T(8,128)S(1)} %fusion.26), custom_call_target="InvertDiagBlocksLowerTriangular" | custom-call | tf_op jit(solution)/shard_map/jvp(jit(_solve_triangular))/vmap()/triangular_solve | solution.py:39
  166.0 3.4 fusion.53
  173.6 23.2 %collective-permute-done.1 = f32[16]{0:T(128)S(1)} collective-permute-done((f32[16]{0:T(128)S(1)}, f32[16]{0:T(128)S(1)}, u32[]{:S(2)}, u32[]{:S(2)}) %collective-permute-start.1) | collective-permute-done | bytes 96 | tf_op jit(solution)/shard_map/ppermute | solution.py:13
  196.8 3.0 collective-permute-start.3
  205.5 3.3 collective-permute-start.7
  212.2 3.4 collective-permute-start.2
  215.6 19.5 %collective-permute-done.2 = f32[16,128,128]{2,1,0:T(8,128)S(1)} collective-permute-done((f32[16,128,128]{2,1,0:T(8,128)S(1)}, f32[16,128,128]{2,1,0:T(8,128)S(1)}, u32[]{:S(2)}, u32[]{:S(2)}) %collective-permute-start.2) | collective-permute-done | bytes 1048608 | tf_op jit(solution)/shard_map/ppermute | solution.py:13
  241.9 16.2 %collective-permute-done.4 = f32[16,128,128]{2,1,0:T(8,128)} collective-permute-done((f32[16,128,128]{2,1,0:T(8,128)}, f32[16,128,128]{2,1,0:T(8,128)}, u32[]{:S(2)}, u32[]{:S(2)}) %collective-permute-start.4) | collective-permute-done | bytes 1048608 | tf_op jit(solution)/shard_map/ppermute | solution.py:13
  264.7 37.0 %collective-permute-done.6 = f32[16,128,128]{2,1,0:T(8,128)S(1)} collective-permute-done((f32[16,128,128]{2,1,0:T(8,128)S(1)}, f32[16,128,128]{2,1,0:T(8,128)S(1)}, u32[]{:S(2)}, u32[]{:S(2)}) %collective-permute-start.6) | collective-permute-done | bytes 1048608 | tf_op jit(solution)/shard_map/ppermute | solution.py:13
  301.9 6.1 collective-permute-start.8
  309.7 42.9 %collective-permute-done.8 = f32[16,128,128]{2,1,0:T(8,128)S(1)} collective-permute-done((f32[16,128,128]{2,1,0:T(8,128)S(1)}, f32[16,128,128]{2,1,0:T(8,128)S(1)}, u32[]{:S(2)}, u32[]{:S(2)}) %collective-permute-start.8) | collective-permute-done | bytes 1048608 | tf_op jit(solution)/shard_map/ppermute | solution.py:13
  352.8 8.4 %fusion.1 = (f32[16,128,128]{1,2,0:T(8,128)S(1)}, f32[16,5,128,128]{3,2,1,0:T(8,128)S(1)}) fusion(f32[16,128,5]{1,2,0:T(8,128)S(1)} %copy.121, f32[16,128,128]{1,2,0:T(8,128)S(1)} %bitcast.208, f32[16,128]{1,0:T(8,128)S(1)} %add_rsqrt_fusion.1, f32[5,16,128,128]{3,2,1,0:T(8,128)S(1)} %bitcast_dynamic-update-slice_fusion), kind=kOutput, calls=%fused_computation.3 | convolution fusion | flops 2015887360 | bytes 12632064 | tf_op jit(solution)/shard_map/jvp(htk,lhkv->lhtv)/dot_general | solution.py:65
  365.7 6.1 fusion.8
  372.1 3.5 collective-permute-start.10
  378.1 35.8 %collective-permute-done.9 = f32[16]{0:T(128)S(1)} collective-permute-done((f32[16]{0:T(128)S(1)}, f32[16]{0:T(128)S(1)}, u32[]{:S(2)}, u32[]{:S(2)}) %collective-permute-start.9) | collective-permute-done | bytes 96 | tf_op jit(solution)/shard_map/ppermute | solution.py:13
  414.5 35.2 %collective-permute-done.11 = f32[16,128,128]{2,1,0:T(8,128)S(1)} collective-permute-done((f32[16,128,128]{2,1,0:T(8,128)S(1)}, f32[16,128,128]{2,1,0:T(8,128)S(1)}, u32[]{:S(2)}, u32[]{:S(2)}) %collective-permute-start.11) | collective-permute-done | bytes 1048608 | tf_op jit(solution)/shard_map/ppermute | solution.py:13
  451.3 6.0 collective-permute-start.12
  459.4 21.3 %collective-permute-done.12 = f32[16,128,128]{2,1,0:T(8,128)S(1)} collective-permute-done((f32[16,128,128]{2,1,0:T(8,128)S(1)}, f32[16,128,128]{2,1,0:T(8,128)S(1)}, u32[]{:S(2)}, u32[]{:S(2)}) %collective-permute-start.12) | collective-permute-done | bytes 1048608 | tf_op jit(solution)/shard_map/ppermute | solution.py:13
  482.0 3.0 collective-permute-start.13
  487.4 6.1 multiply_reduce_fusion.3
  496.5 79.0 %psum.7 = f32[128]{0:T(128)} all-reduce(f32[128]{0:T(128)S(1)} %get-tuple-element.22), channel_id=1, replica_groups=mesh['ctx'=32,'rep'=8] {'ctx'}, use_global_device_ids=true, to_apply=%region_11.13 | all-reduce | flops 128 | bytes 1024 | tf_op jit(solution)/shard_map/psum | solution.py:157
  575.5 2.8 fusion.36
  583.9 9.7 %collective-permute-done.14 = f32[16,128,128]{2,1,0:T(8,128)S(1)} collective-permute-done((f32[16,128,128]{2,1,0:T(8,128)S(1)}, f32[16,128,128]{2,1,0:T(8,128)S(1)}, u32[]{:S(2)}, u32[]{:S(2)}) %collective-permute-start.14) | collective-permute-done | bytes 1048608 | tf_op jit(solution)/shard_map/ppermute | solution.py:13
  606.2 2.7 multiply_reduce_fusion.2
  (129 shorter events, 75.8 us)
Async XLA Ops:
  2.2 169.4 %copy-start.8 = (f32[128,16,128]{2,0,1:T(8,128)}, f32[128,16,128]{2,0,1:T(8,128)S(1)}, u32[]{:S(2)}) copy-start(f32[128,16,128]{2,0,1:T(8,128)S(1)} %copy.57) | copy-start | bytes 3145732
  169.4 70.1 %copy-start.18 = (f32[128,16,6]{0,1,2:T(8,128)S(1)}, f32[128,16,6]{0,1,2:T(8,128)}, u32[]{:S(2)}) copy-start(f32[128,16,6]{0,1,2:T(8,128)} %param.16) | copy-start | bytes 147460
  171.6 38.7 %collective-permute-start = (f32[16,128,128]{2,1,0:T(8,128)}, f32[16,128,128]{2,1,0:T(8,128)}, u32[]{:S(2)}, u32[]{:S(2)}) collective-permute-start(f32[16,128,128]{2,1,0:T(8,128)} %fusion.63), channel_id=1, source_target_pairs={{0,8},{8,0},{16,24},{24,16},{32,40},{40,32},{48,56},{56,48},{64,72... | collective-permute-start | bytes 3145736 | tf_op jit(solution)/shard_map/ppermute | solution.py:13
  173.1 23.7 %collective-permute-start.1 = (f32[16]{0:T(128)S(1)}, f32[16]{0:T(128)S(1)}, u32[]{:S(2)}, u32[]{:S(2)}) collective-permute-start(f32[16]{0:T(128)S(1)} %slice_reduce_fusion), channel_id=1, source_target_pairs={{0,8},{8,0},{16,24},{24,16},{32,40},{40,32},{48,56},{56,48},{64,72... | collective-permute-start | bytes 200 | tf_op jit(solution)/shard_map/ppermute | solution.py:13
  196.8 5.1 collective-permute-start.3
  201.9 3.6 collective-permute-start.5
  205.5 4.8 collective-permute-start.7
  212.2 22.9 %collective-permute-start.2 = (f32[16,128,128]{2,1,0:T(8,128)S(1)}, f32[16,128,128]{2,1,0:T(8,128)S(1)}, u32[]{:S(2)}, u32[]{:S(2)}) collective-permute-start(f32[16,128,128]{2,1,0:T(8,128)S(1)} %add_select_fusion.4), channel_id=1, source_target_pairs={{0,16},{8,24},{16,0},{24,8},{32,48},{40,56},{48,32},{56,40},{64,80... | collective-permute-start | bytes 3145736 | tf_op jit(solution)/shard_map/ppermute | solution.py:13
  235.1 27.4 %copy-start.19 = (f32[64,128]{1,0:T(8,128)S(1)}, f32[64,128]{1,0:T(8,128)}, u32[]{:S(2)}) copy-start(f32[64,128]{1,0:T(8,128)} %param.19) | copy-start | bytes 98308
  236.5 21.6 %collective-permute-start.4 = (f32[16,128,128]{2,1,0:T(8,128)}, f32[16,128,128]{2,1,0:T(8,128)}, u32[]{:S(2)}, u32[]{:S(2)}) collective-permute-start(f32[16,128,128]{2,1,0:T(8,128)} %add_select_fusion.3), channel_id=1, source_target_pairs={{0,32},{8,40},{16,48},{24,56},{32,0},{40,8},{48,16},{56,24},{64,96... | collective-permute-start | bytes 3145736 | tf_op jit(solution)/shard_map/ppermute | solution.py:13
  259.9 48.2 %copy-start.16 = (f32[16,128,128]{2,1,0:T(8,128)S(1)}, f32[16,128,128]{2,1,0:T(8,128)}, u32[]{:S(2)}) copy-start(f32[16,128,128]{2,1,0:T(8,128)} %copy-done.15) | copy-start | bytes 3145732
  259.9 41.7 %collective-permute-start.6 = (f32[16,128,128]{2,1,0:T(8,128)S(1)}, f32[16,128,128]{2,1,0:T(8,128)S(1)}, u32[]{:S(2)}, u32[]{:S(2)}) collective-permute-start(f32[16,128,128]{2,1,0:T(8,128)S(1)} %add_select_fusion.2), channel_id=1, source_target_pairs={{0,64},{8,72},{16,80},{24,88},{32,96},{40,104},{48,112},{56,120},{... | collective-permute-start | bytes 3145736 | tf_op jit(solution)/shard_map/ppermute | solution.py:13
  264.6 96.6 %copy-start.4 = (f32[16,128,128]{2,1,0:T(8,128)}, f32[16,128,128]{2,1,0:T(8,128)S(1)}, u32[]{:S(2)}) copy-start(f32[16,128,128]{2,1,0:T(8,128)S(1)} %convolution_multiply_fusion.1) | copy-start | bytes 3145732
  301.9 50.8 %collective-permute-start.8 = (f32[16,128,128]{2,1,0:T(8,128)S(1)}, f32[16,128,128]{2,1,0:T(8,128)S(1)}, u32[]{:S(2)}, u32[]{:S(2)}) collective-permute-start(f32[16,128,128]{2,1,0:T(8,128)S(1)} %add_select_fusion.1), channel_id=1, source_target_pairs={{0,128},{8,136},{16,144},{24,152},{32,160},{40,168},{48,176},{56,1... | collective-permute-start | bytes 3145736 | tf_op jit(solution)/shard_map/ppermute | solution.py:13
  363.9 123.4 %copy-start = (f32[16,128,128]{1,2,0:T(8,128)}, f32[16,128,128]{1,2,0:T(8,128)S(1)}, u32[]{:S(2)}) copy-start(f32[16,128,128]{1,2,0:T(8,128)S(1)} %get-tuple-element.25) | copy-start | bytes 3145732
  371.9 108.8 %copy-start.2 = (f32[5,16,128,128]{3,2,1,0:T(8,128)}, f32[5,16,128,128]{3,2,1,0:T(8,128)S(1)}, u32[]{:S(2)}) copy-start(f32[5,16,128,128]{3,2,1,0:T(8,128)S(1)} %fusion.8) | copy-start | bytes 15728644
  372.1 41.9 %collective-permute-start.10 = (f32[16,128,128]{2,1,0:T(8,128)S(1)}, f32[16,128,128]{2,1,0:T(8,128)S(1)}, u32[]{:S(2)}, u32[]{:S(2)}) collective-permute-start(f32[16,128,128]{2,1,0:T(8,128)S(1)} %fusion.48), channel_id=1, source_target_pairs={{0,128},{8,136},{16,144},{24,152},{32,160},{40,168},{48,176},{56,1... | collective-permute-start | bytes 3145736 | tf_op jit(solution)/shard_map/ppermute | solution.py:13
  375.6 38.3 %collective-permute-start.9 = (f32[16]{0:T(128)S(1)}, f32[16]{0:T(128)S(1)}, u32[]{:S(2)}, u32[]{:S(2)}) collective-permute-start(f32[16]{0:T(128)S(1)} %get-tuple-element.31), channel_id=1, source_target_pairs={{0,128},{8,136},{16,144},{24,152},{32,160},{40,168},{48,176},{56,1... | collective-permute-start | bytes 200 | tf_op jit(solution)/shard_map/ppermute | solution.py:13
  414.4 35.3 %collective-permute-start.11 = (f32[16,128,128]{2,1,0:T(8,128)S(1)}, f32[16,128,128]{2,1,0:T(8,128)S(1)}, u32[]{:S(2)}, u32[]{:S(2)}) collective-permute-start(f32[16,128,128]{2,1,0:T(8,128)S(1)} %fusion.45), channel_id=1, source_target_pairs={{0,64},{8,72},{16,80},{24,88},{32,96},{40,104},{48,112},{56,120},{... | collective-permute-start | bytes 3145736 | tf_op jit(solution)/shard_map/ppermute | solution.py:13
  451.3 36.1 %copy-start.11 = (f32[16,128,128]{2,1,0:T(8,128)}, f32[16,128,128]{2,1,0:T(8,128)S(1)}, u32[]{:S(2)}) copy-start(f32[16,128,128]{2,1,0:T(8,128)S(1)} %get-tuple-element.29) | copy-start | bytes 3145732
  451.3 29.3 %collective-permute-start.12 = (f32[16,128,128]{2,1,0:T(8,128)S(1)}, f32[16,128,128]{2,1,0:T(8,128)S(1)}, u32[]{:S(2)}, u32[]{:S(2)}) collective-permute-start(f32[16,128,128]{2,1,0:T(8,128)S(1)} %get-tuple-element.28), channel_id=1, source_target_pairs={{0,32},{8,40},{16,48},{24,56},{32,0},{40,8},{48,16},{56,24},{64,96... | collective-permute-start | bytes 3145736 | tf_op jit(solution)/shard_map/ppermute | solution.py:13
  459.4 25.7 %copy-start.6 = (f32[16,128,128]{2,1,0:T(8,128)}, f32[16,128,128]{2,1,0:T(8,128)S(1)}, u32[]{:S(2)}) copy-start(f32[16,128,128]{2,1,0:T(8,128)S(1)} %convolution_multiply_fusion) | copy-start | bytes 3145732
  482.0 93.4 %collective-permute-start.13 = (f32[16,128,128]{2,1,0:T(8,128)}, f32[16,128,128]{2,1,0:T(8,128)}, u32[]{:S(2)}, u32[]{:S(2)}) collective-permute-start(f32[16,128,128]{2,1,0:T(8,128)} %fusion.39), channel_id=1, source_target_pairs={{0,16},{8,24},{16,0},{24,8},{32,48},{40,56},{48,32},{56,40},{64,80... | collective-permute-start | bytes 3145736 | tf_op jit(solution)/shard_map/ppermute | solution.py:13
  578.3 15.3 %collective-permute-start.14 = (f32[16,128,128]{2,1,0:T(8,128)S(1)}, f32[16,128,128]{2,1,0:T(8,128)S(1)}, u32[]{:S(2)}, u32[]{:S(2)}) collective-permute-start(f32[16,128,128]{2,1,0:T(8,128)S(1)} %get-tuple-element.26), channel_id=1, source_target_pairs={{0,8},{8,0},{16,24},{24,16},{32,40},{40,32},{48,56},{56,48},{64,72... | collective-permute-start | bytes 3145736 | tf_op jit(solution)/shard_map/ppermute | solution.py:13
  (13 other events, 82.2 us)
where the time goes:
time: 622 us; the launch traced here: 613 us
  waiting for transfers between devices  246 us (40%)
  other arithmetic  178 us (29%)
  blocking collectives  79 us (13%)
  matrix products  54.6 us (9%)
  starting transfers between devices  39.7 us (6%)
  local copies, waits for them, and re-layouts  13.7 us (2%)
    ppermute x15, waiting for transfers between devices, from_partner(): return lax.ppermute(value, axis, pairs)  246 us
    another operation x2, other arithmetic, prepare(): jax.scipy.linalg.solve_triangular(system, beta_heads[:, :, None] * value_...  159 us
    psum x1, blocking collectives, local(): grad_gain = lax.psum(grad_gain_local, 'ctx')  79 us
    ppermute x15, starting transfers between devices, from_partner(): return lax.ppermute(value, axis, pairs)  39.7 us
    dot_general x3, matrix products, finish(): jnp.einsum('htk,lhkv->lhtv', query_normed, bucket_states, precision=topmo...  20.6 us
  transfers between devices with their start and end apart: 15, of which 12 were waited for; matrix products, arithmetic and copies ran while one was open for 4% of the time, Pallas kernels for 0%

commit v1 on v0

--- a/solution.py
+++ b/solution.py
@@ -154,7 +154,7 @@
     grad_query, grad_key, grad_value, grad_beta = prepare_back(
         (grad_qnormed, grad_knormed, grad_pseudo, adjoint)
     )
-    grad_gain = lax.psum(grad_gain_local, "ctx")
+    grad_gain = jnp.sum(lax.all_gather(grad_gain_local, "ctx"), axis=0)
     return (
         grad_query.astype(jnp.bfloat16),
         grad_key.astype(jnp.bfloat16),

time: 622 us -> 591 us (0.950)
  blocking collectives: 79 us -> 45.1 us
    psum x1 -> x0, blocking collectives: 79 us -> none  [local(): grad_gain = lax.psum(grad_gain_local, 'ctx')]
    all_gather x0 -> x1, blocking collectives: none -> 45.1 us  [local(): grad_gain = jnp.sum(lax.all_gather(grad_gain_local, 'ctx'), axis=0)]
  transfers between devices with their start and end apart: 15 -> 15, of which waited for: 12 -> 12; matrix products, arithmetic and copies ran while one was open for 4% -> 5% of each run, Pallas kernels for 0% -> 0%
where the time goes in v1:
time: 591 us; the launch traced here: 582 us
  waiting for transfers between devices  247 us (42%)
  other arithmetic  180 us (30%)
  matrix products  54.5 us (9%)
  blocking collectives  45.1 us (8%)
  starting transfers between devices  40.8 us (7%)
  local copies, waits for them, and re-layouts  12.7 us (2%)
    ppermute x15, waiting for transfers between devices, from_partner(): return lax.ppermute(value, axis, pairs)  247 us
    another operation x2, other arithmetic, prepare(): jax.scipy.linalg.solve_triangular(system, beta_heads[:, :, None] * value_...  160 us
    all_gather x1, blocking collectives, local(): grad_gain = jnp.sum(lax.all_gather(grad_gain_local, 'ctx'), axis=0)  45.1 us
    ppermute x15, starting transfers between devices, from_partner(): return lax.ppermute(value, axis, pairs)  40.8 us
    dot_general x3, matrix products, finish(): jnp.einsum('htk,lhkv->lhtv', query_normed, bucket_states, precision=topmo...  20.6 us
  transfers between devices with their start and end apart: 15, of which 12 were waited for; matrix products, arithmetic and copies ran while one was open for 5% of the time, Pallas kernels for 0%

profile of v1, /device:TPU:16, one launch (start us, length us, event | category | flops | bytes accessed | tf_op | source)
XLA Modules:
  0.0 581.7 jit_solution(12995912900554145319)
XLA Ops:
  7.9 158.6 %custom-call.7 = f32[16,1,128,128]{2,3,1,0:T(8,128)} custom-call(f32[16,1,128,128]{3,2,1,0:T(8,128)} %fusion.26), custom_call_target="InvertDiagBlocksLowerTriangular" | custom-call | tf_op jit(solution)/shard_map/jvp(jit(_solve_triangular))/vmap()/triangular_solve | solution.py:39
  166.6 3.4 fusion.53
  174.3 23.2 %collective-permute-done.1 = f32[16]{0:T(128)S(1)} collective-permute-done((f32[16]{0:T(128)S(1)}, f32[16]{0:T(128)S(1)}, u32[]{:S(2)}, u32[]{:S(2)}) %collective-permute-start.1) | collective-permute-done | bytes 96 | tf_op jit(solution)/shard_map/ppermute | solution.py:13
  197.5 3.0 collective-permute-start.3
  206.1 3.3 collective-permute-start.7
  212.8 3.4 collective-permute-start.2
  216.2 19.5 %collective-permute-done.2 = f32[16,128,128]{2,1,0:T(8,128)S(1)} collective-permute-done((f32[16,128,128]{2,1,0:T(8,128)S(1)}, f32[16,128,128]{2,1,0:T(8,128)S(1)}, u32[]{:S(2)}, u32[]{:S(2)}) %collective-permute-start.2) | collective-permute-done | bytes 1048608 | tf_op jit(solution)/shard_map/ppermute | solution.py:13
  242.5 16.2 %collective-permute-done.4 = f32[16,128,128]{2,1,0:T(8,128)} collective-permute-done((f32[16,128,128]{2,1,0:T(8,128)}, f32[16,128,128]{2,1,0:T(8,128)}, u32[]{:S(2)}, u32[]{:S(2)}) %collective-permute-start.4) | collective-permute-done | bytes 1048608 | tf_op jit(solution)/shard_map/ppermute | solution.py:13
  265.3 37.0 %collective-permute-done.6 = f32[16,128,128]{2,1,0:T(8,128)S(1)} collective-permute-done((f32[16,128,128]{2,1,0:T(8,128)S(1)}, f32[16,128,128]{2,1,0:T(8,128)S(1)}, u32[]{:S(2)}, u32[]{:S(2)}) %collective-permute-start.6) | collective-permute-done | bytes 1048608 | tf_op jit(solution)/shard_map/ppermute | solution.py:13
  302.5 6.1 %collective-permute-start.8 = (f32[16,128,128]{2,1,0:T(8,128)S(1)}, f32[16,128,128]{2,1,0:T(8,128)S(1)}, u32[]{:S(2)}, u32[]{:S(2)}) collective-permute-start(f32[16,128,128]{2,1,0:T(8,128)S(1)} %add_select_fusion.1), channel_id=1, source_target_pairs={{0,128},{8,136},{16,144},{24,152},{32,160},{40,168},{48,176},{56,1... | collective-permute-start | bytes 3145736 | tf_op jit(solution)/shard_map/ppermute | solution.py:13
  310.3 42.9 %collective-permute-done.8 = f32[16,128,128]{2,1,0:T(8,128)S(1)} collective-permute-done((f32[16,128,128]{2,1,0:T(8,128)S(1)}, f32[16,128,128]{2,1,0:T(8,128)S(1)}, u32[]{:S(2)}, u32[]{:S(2)}) %collective-permute-start.8) | collective-permute-done | bytes 1048608 | tf_op jit(solution)/shard_map/ppermute | solution.py:13
  353.4 8.4 %fusion.1 = (f32[16,128,128]{1,2,0:T(8,128)S(1)}, f32[16,5,128,128]{3,2,1,0:T(8,128)S(1)}) fusion(f32[16,128,5]{1,2,0:T(8,128)S(1)} %copy.158, f32[16,128,128]{1,2,0:T(8,128)S(1)} %bitcast.209, f32[16,128]{1,0:T(8,128)S(1)} %add_rsqrt_fusion.1, f32[5,16,128,128]{3,2,1,0:T(8,128)S(1)} %bitcast_dynamic-update-slice_fusion), kind=kOutput, calls=%fused_computation.3 | convolution fusion | flops 2015887360 | bytes 12632064 | tf_op jit(solution)/shard_map/jvp(htk,lhkv->lhtv)/dot_general | solution.py:65
  366.4 6.1 %fusion.8 = f32[5,16,128,128]{3,2,1,0:T(8,128)S(1)} fusion(f32[16,5,128,128]{3,2,1,0:T(8,128)S(1)} %get-tuple-element.50, f32[16,128,128]{1,2,0:T(8,128)S(1)} %bitcast.210, f32[16,128]{1,0:T(8,128)S(1)} %add_rsqrt_fusion.1), kind=kOutput, calls=%fused_computation.11 | convolution fusion | flops 2013528064 | bytes 11542528 | tf_op jit(solution)/shard_map/transpose(jvp(htk,lhkv->lhtv))/dot_general | solution.py:65
  372.7 3.5 collective-permute-start.10
  378.7 35.8 %collective-permute-done.9 = f32[16]{0:T(128)S(1)} collective-permute-done((f32[16]{0:T(128)S(1)}, f32[16]{0:T(128)S(1)}, u32[]{:S(2)}, u32[]{:S(2)}) %collective-permute-start.9) | collective-permute-done | bytes 96 | tf_op jit(solution)/shard_map/ppermute | solution.py:13
  415.1 35.2 %collective-permute-done.11 = f32[16,128,128]{2,1,0:T(8,128)S(1)} collective-permute-done((f32[16,128,128]{2,1,0:T(8,128)S(1)}, f32[16,128,128]{2,1,0:T(8,128)S(1)}, u32[]{:S(2)}, u32[]{:S(2)}) %collective-permute-start.11) | collective-permute-done | bytes 1048608 | tf_op jit(solution)/shard_map/ppermute | solution.py:13
  451.9 6.0 %collective-permute-start.12 = (f32[16,128,128]{2,1,0:T(8,128)S(1)}, f32[16,128,128]{2,1,0:T(8,128)S(1)}, u32[]{:S(2)}, u32[]{:S(2)}) collective-permute-start(f32[16,128,128]{2,1,0:T(8,128)S(1)} %get-tuple-element.35), channel_id=1, source_target_pairs={{0,32},{8,40},{16,48},{24,56},{32,0},{40,8},{48,16},{56,24},{64,96... | collective-permute-start | bytes 3145736 | tf_op jit(solution)/shard_map/ppermute | solution.py:13
  460.0 21.3 %collective-permute-done.12 = f32[16,128,128]{2,1,0:T(8,128)S(1)} collective-permute-done((f32[16,128,128]{2,1,0:T(8,128)S(1)}, f32[16,128,128]{2,1,0:T(8,128)S(1)}, u32[]{:S(2)}, u32[]{:S(2)}) %collective-permute-start.12) | collective-permute-done | bytes 1048608 | tf_op jit(solution)/shard_map/ppermute | solution.py:13
  482.7 3.0 collective-permute-start.13
  488.0 6.1 %multiply_reduce_fusion.3 = (f32[16,128]{1,0:T(8,128)S(1)}, f32[16,128,128]{1,2,0:T(8,128)S(1)}) fusion(f32[128,2048]{0,1:T(8,128)S(1)} %copy.83, f32[16,128,128]{1,2,0:T(8,128)S(1)} %fusion.77, f32[5,16,128,128]{3,2,1,0:T(8,128)S(1)} %bitcast_dynamic-update-slice_fusion, f32[16,128,5]{1,2,0:T(8,128)S(1)} %copy.158, f32[16,128,128]{1,2,0:T(8,128)S(1)} %get-tuple-element.32), kind=kOutput, calls=%fused_computation.91 | convolution fusion | flops 2015361024 | bytes 9486336 | tf_op jit(solution)/shard_map/transpose(jvp(htk,lhkv->lhtv))/dot_general | solution.py:65
  497.1 45.1 %all-gather.1 = f32[32,1,128]{2,1,0:T(1,128)S(1)} all-gather(f32[1,1,128]{2,1,0:T(1,128)S(1)} %bitcast.232), channel_id=2, replica_groups=mesh['ctx'=32,'rep'=8] {'ctx'}, dimensions={0}, use_global_device_ids=true | all-gather | bytes 16896 | tf_op jit(solution)/shard_map/all_gather | solution.py:157
  542.8 2.8 fusion.36
  552.4 10.2 %collective-permute-done.14 = f32[16,128,128]{2,1,0:T(8,128)S(1)} collective-permute-done((f32[16,128,128]{2,1,0:T(8,128)S(1)}, f32[16,128,128]{2,1,0:T(8,128)S(1)}, u32[]{:S(2)}, u32[]{:S(2)}) %collective-permute-start.14) | collective-permute-done | bytes 1048608 | tf_op jit(solution)/shard_map/ppermute | solution.py:13
  575.2 2.7 multiply_reduce_fusion.2
  (130 shorter events, 77.3 us)
Async XLA Ops:
  2.2 170.0 %copy-start.8 = (f32[128,16,128]{2,0,1:T(8,128)}, f32[128,16,128]{2,0,1:T(8,128)S(1)}, u32[]{:S(2)}) copy-start(f32[128,16,128]{2,0,1:T(8,128)S(1)} %copy.92) | copy-start | bytes 3145732
  6.4 160.2 %copy-start.12 = (f32[16,128,128]{2,1,0:T(8,128)}, f32[16,128,128]{2,1,0:T(8,128)S(1)}, u32[]{:S(2)}) copy-start(f32[16,128,128]{2,1,0:T(8,128)S(1)} %fusion.80) | copy-start | bytes 3145732
  170.0 70.1 %copy-start.18 = (f32[128,16,6]{0,1,2:T(8,128)S(1)}, f32[128,16,6]{0,1,2:T(8,128)}, u32[]{:S(2)}) copy-start(f32[128,16,6]{0,1,2:T(8,128)} %param.16) | copy-start | bytes 147460
  172.2 38.7 %collective-permute-start = (f32[16,128,128]{2,1,0:T(8,128)}, f32[16,128,128]{2,1,0:T(8,128)}, u32[]{:S(2)}, u32[]{:S(2)}) collective-permute-start(f32[16,128,128]{2,1,0:T(8,128)} %fusion.63), channel_id=1, source_target_pairs={{0,8},{8,0},{16,24},{24,16},{32,40},{40,32},{48,56},{56,48},{64,72... | collective-permute-start | bytes 3145736 | tf_op jit(solution)/shard_map/ppermute | solution.py:13
  173.7 23.7 %collective-permute-start.1 = (f32[16]{0:T(128)S(1)}, f32[16]{0:T(128)S(1)}, u32[]{:S(2)}, u32[]{:S(2)}) collective-permute-start(f32[16]{0:T(128)S(1)} %slice_reduce_fusion), channel_id=1, source_target_pairs={{0,8},{8,0},{16,24},{24,16},{32,40},{40,32},{48,56},{56,48},{64,72... | collective-permute-start | bytes 200 | tf_op jit(solution)/shard_map/ppermute | solution.py:13
  197.5 5.1 collective-permute-start.3
  202.5 3.6 collective-permute-start.5
  206.1 4.8 collective-permute-start.7
  212.8 22.9 %collective-permute-start.2 = (f32[16,128,128]{2,1,0:T(8,128)S(1)}, f32[16,128,128]{2,1,0:T(8,128)S(1)}, u32[]{:S(2)}, u32[]{:S(2)}) collective-permute-start(f32[16,128,128]{2,1,0:T(8,128)S(1)} %add_select_fusion.4), channel_id=1, source_target_pairs={{0,16},{8,24},{16,0},{24,8},{32,48},{40,56},{48,32},{56,40},{64,80... | collective-permute-start | bytes 3145736 | tf_op jit(solution)/shard_map/ppermute | solution.py:13
  235.7 27.4 %copy-start.19 = (f32[64,128]{1,0:T(8,128)S(1)}, f32[64,128]{1,0:T(8,128)}, u32[]{:S(2)}) copy-start(f32[64,128]{1,0:T(8,128)} %param.19) | copy-start | bytes 98308
  237.1 21.6 %collective-permute-start.4 = (f32[16,128,128]{2,1,0:T(8,128)}, f32[16,128,128]{2,1,0:T(8,128)}, u32[]{:S(2)}, u32[]{:S(2)}) collective-permute-start(f32[16,128,128]{2,1,0:T(8,128)} %add_select_fusion.3), channel_id=1, source_target_pairs={{0,32},{8,40},{16,48},{24,56},{32,0},{40,8},{48,16},{56,24},{64,96... | collective-permute-start | bytes 3145736 | tf_op jit(solution)/shard_map/ppermute | solution.py:13
  260.5 48.2 %copy-start.16 = (f32[16,128,128]{2,1,0:T(8,128)S(1)}, f32[16,128,128]{2,1,0:T(8,128)}, u32[]{:S(2)}) copy-start(f32[16,128,128]{2,1,0:T(8,128)} %copy-done.15) | copy-start | bytes 3145732
  260.5 41.7 %collective-permute-start.6 = (f32[16,128,128]{2,1,0:T(8,128)S(1)}, f32[16,128,128]{2,1,0:T(8,128)S(1)}, u32[]{:S(2)}, u32[]{:S(2)}) collective-permute-start(f32[16,128,128]{2,1,0:T(8,128)S(1)} %add_select_fusion.2), channel_id=1, source_target_pairs={{0,64},{8,72},{16,80},{24,88},{32,96},{40,104},{48,112},{56,120},{... | collective-permute-start | bytes 3145736 | tf_op jit(solution)/shard_map/ppermute | solution.py:13
  265.2 96.6 %copy-start.4 = (f32[16,128,128]{2,1,0:T(8,128)}, f32[16,128,128]{2,1,0:T(8,128)S(1)}, u32[]{:S(2)}) copy-start(f32[16,128,128]{2,1,0:T(8,128)S(1)} %convolution_multiply_fusion.1) | copy-start | bytes 3145732
  302.5 50.8 %collective-permute-start.8 = (f32[16,128,128]{2,1,0:T(8,128)S(1)}, f32[16,128,128]{2,1,0:T(8,128)S(1)}, u32[]{:S(2)}, u32[]{:S(2)}) collective-permute-start(f32[16,128,128]{2,1,0:T(8,128)S(1)} %add_select_fusion.1), channel_id=1, source_target_pairs={{0,128},{8,136},{16,144},{24,152},{32,160},{40,168},{48,176},{56,1... | collective-permute-start | bytes 3145736 | tf_op jit(solution)/shard_map/ppermute | solution.py:13
  364.5 123.4 %copy-start = (f32[16,128,128]{1,2,0:T(8,128)}, f32[16,128,128]{1,2,0:T(8,128)S(1)}, u32[]{:S(2)}) copy-start(f32[16,128,128]{1,2,0:T(8,128)S(1)} %get-tuple-element.32) | copy-start | bytes 3145732
  372.5 108.8 %copy-start.2 = (f32[5,16,128,128]{3,2,1,0:T(8,128)}, f32[5,16,128,128]{3,2,1,0:T(8,128)S(1)}, u32[]{:S(2)}) copy-start(f32[5,16,128,128]{3,2,1,0:T(8,128)S(1)} %fusion.8) | copy-start | bytes 15728644
  372.7 41.8 %collective-permute-start.10 = (f32[16,128,128]{2,1,0:T(8,128)S(1)}, f32[16,128,128]{2,1,0:T(8,128)S(1)}, u32[]{:S(2)}, u32[]{:S(2)}) collective-permute-start(f32[16,128,128]{2,1,0:T(8,128)S(1)} %fusion.48), channel_id=1, source_target_pairs={{0,128},{8,136},{16,144},{24,152},{32,160},{40,168},{48,176},{56,1... | collective-permute-start | bytes 3145736 | tf_op jit(solution)/shard_map/ppermute | solution.py:13
  376.3 38.3 %collective-permute-start.9 = (f32[16]{0:T(128)S(1)}, f32[16]{0:T(128)S(1)}, u32[]{:S(2)}, u32[]{:S(2)}) collective-permute-start(f32[16]{0:T(128)S(1)} %get-tuple-element.38), channel_id=1, source_target_pairs={{0,128},{8,136},{16,144},{24,152},{32,160},{40,168},{48,176},{56,1... | collective-permute-start | bytes 200 | tf_op jit(solution)/shard_map/ppermute | solution.py:13
  415.0 35.4 %collective-permute-start.11 = (f32[16,128,128]{2,1,0:T(8,128)S(1)}, f32[16,128,128]{2,1,0:T(8,128)S(1)}, u32[]{:S(2)}, u32[]{:S(2)}) collective-permute-start(f32[16,128,128]{2,1,0:T(8,128)S(1)} %fusion.45), channel_id=1, source_target_pairs={{0,64},{8,72},{16,80},{24,88},{32,96},{40,104},{48,112},{56,120},{... | collective-permute-start | bytes 3145736 | tf_op jit(solution)/shard_map/ppermute | solution.py:13
  451.9 36.1 %copy-start.11 = (f32[16,128,128]{2,1,0:T(8,128)}, f32[16,128,128]{2,1,0:T(8,128)S(1)}, u32[]{:S(2)}) copy-start(f32[16,128,128]{2,1,0:T(8,128)S(1)} %get-tuple-element.36) | copy-start | bytes 3145732
  451.9 29.4 %collective-permute-start.12 = (f32[16,128,128]{2,1,0:T(8,128)S(1)}, f32[16,128,128]{2,1,0:T(8,128)S(1)}, u32[]{:S(2)}, u32[]{:S(2)}) collective-permute-start(f32[16,128,128]{2,1,0:T(8,128)S(1)} %get-tuple-element.35), channel_id=1, source_target_pairs={{0,32},{8,40},{16,48},{24,56},{32,0},{40,8},{48,16},{56,24},{64,96... | collective-permute-start | bytes 3145736 | tf_op jit(solution)/shard_map/ppermute | solution.py:13
  482.7 60.2 %collective-permute-start.13 = (f32[16,128,128]{2,1,0:T(8,128)}, f32[16,128,128]{2,1,0:T(8,128)}, u32[]{:S(2)}, u32[]{:S(2)}) collective-permute-start(f32[16,128,128]{2,1,0:T(8,128)} %fusion.39), channel_id=1, source_target_pairs={{0,16},{8,24},{16,0},{24,8},{32,48},{40,56},{48,32},{56,40},{64,80... | collective-permute-start | bytes 3145736 | tf_op jit(solution)/shard_map/ppermute | solution.py:13
  545.7 16.9 %collective-permute-start.14 = (f32[16,128,128]{2,1,0:T(8,128)S(1)}, f32[16,128,128]{2,1,0:T(8,128)S(1)}, u32[]{:S(2)}, u32[]{:S(2)}) collective-permute-start(f32[16,128,128]{2,1,0:T(8,128)S(1)} %get-tuple-element.33), channel_id=1, source_target_pairs={{0,8},{8,0},{16,24},{24,16},{32,40},{40,32},{48,56},{56,48},{64,72... | collective-permute-start | bytes 3145736 | tf_op jit(solution)/shard_map/ppermute | solution.py:13
  (13 other events, 110.2 us)
